TPU v7x, 128 devices: a whole 4x4x4 slice. The times are simulated.
128 devices in a mesh: seq: 16 (over z, y_hi, core), col: 4 (over x), batch: 2 (over y_lo).
Axes of the slice: x: 4, y: 4 (y_hi: 2, y_lo: 2; y = y_hi * 2 + y_lo), z: 4, core: 2. Of those that a mesh axis runs over, the one named last changes fastest.
Arguments:
- tokens: int32 [2, 1048576], P('batch', ('seq', 'col')), may hold values from 0 to 3
- stem_weight: bfloat16 [64, 768], replicated, may hold values from -1.5 to 1.5
- conv_weight: bfloat16 [3840, 768], replicated, may hold values from -0.09375 to 0.09375
- conv_bias: float32 [768], replicated, may hold values from -1 to 1
- up_weight: bfloat16 [768, 1536], replicated, may hold values from -0.21875 to 0.21875
- norm_gain: float32 [1536], replicated, may hold values from 0.1 to 1.9
- pair_weight: bfloat16 [1536, 64], replicated, may hold values from -0.15625 to 0.15625
- out_weight: bfloat16 [1024, 128], replicated, may hold values from -0.1875 to 0.1875
- cotangent: bfloat16 [2, 512, 512, 128], P('batch', 'seq', 'col'), may hold values from -24 to 24
- projection: float32 [768, 128], replicated, may hold values from -0.21875 to 0.21875
- buckets: int32 [3840], replicated, may hold values from 0 to 31
Outputs:
- input_grad: bfloat16 [2, 65536, 768], P('batch', ('seq', 'col'))
- embedding: float32 [2, 32, 128], P('batch')
All inputs are finite; a program needn't handle non-finite values.
Results may differ from a plain program's by a relative error of at most 0.012.
Values may be sent and summed in bfloat16 or wider, within the bound.
No kernel may reach another device: no remote copies, remote signals or barrier semaphores. Data moves between devices by JAX's collectives and lax.ppermute only.
A program may use at most 128 MiB of HBM per device.

v0:
```python
import jax
import jax.numpy as jnp
from jax import lax
from jax.sharding import PartitionSpec as P

OP = 32
PATCH = 16
POOL = 128
BUCKETS = 32
highest = lax.Precision.HIGHEST


def extended(cells, sides, width):
    for axis, dim in sides:
        count = lax.axis_size(axis)
        ends = count - 1
        head = lax.slice_in_dim(cells, 0, width, axis=dim)
        tail = lax.slice_in_dim(cells, cells.shape[dim] - width, cells.shape[dim], axis=dim)
        cells = jnp.concatenate(
            [
                lax.ppermute(tail, axis, [(i, (i + 1) % count) for i in range(ends)]),
                cells,
                lax.ppermute(head, axis, [((i + 1) % count, i) for i in range(ends)]),
            ],
            axis=dim,
        )
    return cells


def shards(
    tokens,
    stem_weight,
    conv_weight,
    conv_bias,
    up_weight,
    norm_gain,
    pair_weight,
    out_weight,
    cotangent,
    projection,
    buckets,
):
    channels = conv_weight.shape[1]
    kernel = conv_weight.shape[0] // channels
    reach = (kernel - 1) // 2
    patches = tokens.shape[1] // PATCH
    bins_dev = patches // POOL
    bases = tokens[0].reshape(patches, PATCH)
    onehot = (
        (bases[:, :, None] == jnp.arange(4, dtype=jnp.int32))
        .astype(jnp.bfloat16)
        .reshape(patches, PATCH * 4)
    )
    embedded = jnp.dot(onehot, stem_weight, preferred_element_type=jnp.float32).astype(jnp.bfloat16)
    padded = extended(embedded, ((("seq", "col"), 0),), reach)
    unfolded = jnp.concatenate(
        [padded[offset : offset + patches] for offset in range(kernel)], axis=1
    )
    before = jnp.dot(unfolded, conv_weight, preferred_element_type=jnp.float32) + conv_bias
    after, gelu_back = jax.vjp(jax.nn.gelu, before)
    pooled = jnp.mean(after.reshape(bins_dev, POOL, channels), axis=1).astype(jnp.bfloat16)
    hidden = jnp.dot(pooled, up_weight, preferred_element_type=jnp.float32)
    inverse = lax.rsqrt(jnp.mean(hidden * hidden, axis=1, keepdims=True) + 1e-06)
    normed = (hidden * inverse * norm_gain).astype(jnp.bfloat16)
    seq_count = lax.axis_size("seq")
    col_count = lax.axis_size("col")
    row_len = bins_dev * col_count
    col_len = bins_dev * seq_count
    all_bins = row_len * seq_count
    row_index = lax.axis_index("seq")
    col_index = lax.axis_index("col")
    every = lax.all_gather(normed, ("seq", "col"), axis=0, tiled=True)
    row_part = lax.dynamic_slice_in_dim(every, row_index * row_len, row_len, 0)
    col_part = lax.dynamic_slice_in_dim(every, col_index * col_len, col_len, 0)
    left = jnp.dot(row_part, pair_weight[:, :OP], preferred_element_type=jnp.float32).astype(
        jnp.bfloat16
    )
    right = jnp.dot(col_part, pair_weight[:, OP:], preferred_element_type=jnp.float32).astype(
        jnp.bfloat16
    )
    pair_channels = cotangent.shape[3]
    blocks = cotangent[0].reshape(col_count, bins_dev, col_len, pair_channels)
    left_groups = left.astype(jnp.float32).reshape(col_count, bins_dev, OP)
    right_wide = right.astype(jnp.float32)

    def pair_step(carry, inputs):
        block, rows_left = inputs
        outer_grad = lax.dot_general(
            block.reshape(bins_dev * col_len, pair_channels),
            out_weight,
            (((1,), (1,)), ((), ())),
            preferred_element_type=jnp.float32,
        ).reshape(bins_dev, col_len, OP, OP)
        grad_left = jnp.einsum("ijkl,jl->ik", outer_grad, right_wide, precision=highest)
        carry = carry + jnp.einsum("ijkl,ik->jl", outer_grad, rows_left, precision=highest)
        return (carry, grad_left)

    grad_right, grad_left = lax.scan(
        pair_step, jnp.zeros((col_len, OP), jnp.float32), (blocks, left_groups)
    )
    grad_left = grad_left.reshape(row_len, OP)
    row_term = lax.dot_general(
        grad_left,
        pair_weight[:, :OP].astype(jnp.float32),
        (((1,), (1,)), ((), ())),
        precision=highest,
    )
    col_term = lax.dot_general(
        grad_right,
        pair_weight[:, OP:].astype(jnp.float32),
        (((1,), (1,)), ((), ())),
        precision=highest,
    )
    empty_rows = jnp.zeros((all_bins, row_term.shape[1]), jnp.float32)
    placed = lax.dynamic_update_slice_in_dim(
        empty_rows, row_term, row_index * row_len, 0
    ) + lax.dynamic_update_slice_in_dim(empty_rows, col_term, col_index * col_len, 0)
    d_normed = lax.psum_scatter(placed, ("seq", "col"), scatter_dimension=0, tiled=True)
    scaled = d_normed * norm_gain
    inner = jnp.mean(scaled * hidden, axis=1, keepdims=True)
    d_hidden = inverse * scaled - hidden * inverse**3 * inner
    d_pooled = lax.dot_general(
        d_hidden, up_weight.astype(jnp.float32), (((1,), (1,)), ((), ())), precision=highest
    )
    spread = jnp.broadcast_to(d_pooled[:, None, :] / POOL, (bins_dev, POOL, channels)).reshape(
        patches, channels
    )
    d_before = gelu_back(spread)[0].astype(jnp.bfloat16)
    grads_padded = extended(d_before, ((("seq", "col"), 0),), reach)
    stacked = jnp.stack(
        [
            grads_padded[2 * reach - offset : 2 * reach - offset + patches]
            for offset in range(kernel)
        ],
        axis=1,
    )
    input_grad = jnp.einsum(
        "tko,kio->ti",
        stacked,
        conv_weight.reshape(kernel, channels, channels),
        preferred_element_type=jnp.float32,
    ).astype(jnp.bfloat16)
    share_rows = unfolded.shape[1] // lax.axis_size(("seq", "col"))
    share = lax.psum_scatter(
        lax.dot_general(
            unfolded, d_before, (((0,), (0,)), ((), ())), preferred_element_type=jnp.float32
        ),
        ("seq", "col"),
        scatter_dimension=0,
        tiled=True,
    )
    labels = lax.dynamic_slice_in_dim(
        buckets, lax.axis_index(("seq", "col")) * share_rows, share_rows, 0
    )
    projected = jnp.dot(share, projection, precision=highest)
    member = (labels[None, :] == jnp.arange(BUCKETS, dtype=jnp.int32)[:, None]).astype(jnp.float32)
    sketch = lax.psum(jnp.dot(member, projected, precision=highest), ("seq", "col"))
    unit = sketch * lax.rsqrt(jnp.mean(sketch * sketch) + 1e-06)
    center = lax.psum(unit, "batch") / lax.axis_size("batch")
    return (input_grad[None], (unit - center)[None])


def solution(mesh):
    in_specs = (
        P("batch", ("seq", "col")),
        P(),
        P(),
        P(),
        P(),
        P(),
        P(),
        P(),
        P("batch", "seq", "col", None),
        P(),
        P(),
    )
    out_specs = (P("batch", ("seq", "col"), None), P("batch", None, None))
    return jax.shard_map(shards, mesh=mesh, in_specs=in_specs, out_specs=out_specs, check_vma=False)
```

profile of v0, /device:TPU:8, one launch (start us, length us, event | category | flops | bytes accessed | tf_op | source)
XLA Modules:
  0.0 925.7 jit_solution(1880735338173199356)
XLA Ops:
  11.8 3.4 collective-permute-start
  21.5 8.4 bitcast_reduce_fusion
  31.4 72.0 %all-gather.2.cloned.1.call-done = bf16[512,1536]{1,0:T(8,128)(2,1)} async-done(((bf16[8,1536]{1,0:T(8,128)(2,1)}), bf16[512,1536]{1,0:T(8,128)(2,1)}) %all-gather.2.cloned.1.call-update) | async-done | bytes 1572880 | tf_op jit(solution)/shard_map/all_gather | solution.py:72
  105.8 78.4 %while.13 = (s32[]{:T(128)}, f32[128,32]{1,0:T(8,128)S(1)}, f32[4,8,32]{2,1,0:T(8,128)S(1)}, bf16[4,8,128,128]{3,2,1,0:T(8,128)(2,1)}, bf16[1024,128]{1,0:T(8,12...) while((s32[]{:T(128)}, f32[128,32]{1,0:T(8,128)S(1)}, ...), condition=%wide.region_3.4_spmd.clone, body=%wide.region_2.3_spmd.clone.sunk | while | flops 293609472 | bytes 30050948 | solution.py:98
  105.8 3.6 fusion.101
  109.5 11.1 %fusion.102 = f32[1,8,32,1]{2,0,3,1:T(1,128)S(1)} fusion(f32[128,32,1,1]{0,2,1,3:T(1,128)S(1)} %copy.35, f32[8,128,32,32]{1,3,2,0:T(8,128)} %fusion.101), kind=kOutput, calls=%fused_computation.clone.1 | convolution fusion | flops 12582912 | bytes 4211712 | tf_op jit(solution)/shard_map/while/body/eval_jaxpr/ijkl,jl->ik/dot_general | solution.py:94
  120.6 4.7 fusion.103
  125.4 3.6 fusion.101
  129.1 11.1 %fusion.102 = f32[1,8,32,1]{2,0,3,1:T(1,128)S(1)} fusion(f32[128,32,1,1]{0,2,1,3:T(1,128)S(1)} %copy.35, f32[8,128,32,32]{1,3,2,0:T(8,128)} %fusion.101), kind=kOutput, calls=%fused_computation.clone.1 | convolution fusion | flops 12582912 | bytes 4211712 | tf_op jit(solution)/shard_map/while/body/eval_jaxpr/ijkl,jl->ik/dot_general | solution.py:94
  140.2 4.7 fusion.103
  145.0 3.6 fusion.101
  148.7 11.1 %fusion.102 = f32[1,8,32,1]{2,0,3,1:T(1,128)S(1)} fusion(f32[128,32,1,1]{0,2,1,3:T(1,128)S(1)} %copy.35, f32[8,128,32,32]{1,3,2,0:T(8,128)} %fusion.101), kind=kOutput, calls=%fused_computation.clone.1 | convolution fusion | flops 12582912 | bytes 4211712 | tf_op jit(solution)/shard_map/while/body/eval_jaxpr/ijkl,jl->ik/dot_general | solution.py:94
  159.8 4.7 fusion.103
  164.6 3.6 fusion.101
  168.3 11.1 %fusion.102 = f32[1,8,32,1]{2,0,3,1:T(1,128)S(1)} fusion(f32[128,32,1,1]{0,2,1,3:T(1,128)S(1)} %copy.35, f32[8,128,32,32]{1,3,2,0:T(8,128)} %fusion.101), kind=kOutput, calls=%fused_computation.clone.1 | convolution fusion | flops 12582912 | bytes 4211712 | tf_op jit(solution)/shard_map/while/body/eval_jaxpr/ijkl,jl->ik/dot_general | solution.py:94
  179.4 4.7 fusion.103
  191.7 143.6 %reduce-scatter.4.cloned.1.call-done = f32[8,1536]{1,0:T(8,128)} async-done(((f32[512,1536]{1,0:T(8,128)}), f32[8,1536]{1,0:T(8,128)}) %reduce-scatter.4.cloned.1.call-update) | async-done | bytes 49168 | tf_op jit(solution)/shard_map/reduce_scatter | solution.py:118
  339.0 3.7 fusion.15
  342.7 12.6 %fusion.70 = f32[3840,768]{1,0:T(8,128)} fusion(bf16[1024,3840]{1,0:T(8,128)(2,1)} %copy-done.6, bf16[1024,768]{1,0:T(8,128)(2,1)S(1)} %fusion.15), kind=kOutput, calls=%fused_computation.110 | convolution fusion | flops 6039797760 | bytes 21233664 | tf_op jit(solution)/shard_map/dot_general | solution.py:145
  356.6 201.8 %fusion = f32[64,768]{1,0:T(8,128)S(1)} fusion(f32[3840,768]{1,0:T(8,128)} %fusion.70), kind=kCustom, calls=%all-reduce-scatter | all-reduce-scatter fusion | flops 3145729 | bytes 11993600
  569.6 7.4 fusion.36
  578.4 4.3 concatenate.26
  584.2 323.5 %psum.14 = f32[32,128]{1,0:T(8,128)S(1)} all-reduce(f32[32,128]{1,0:T(8,128)S(1)} %fusion.60), channel_id=1, replica_groups=mesh['seq'=16,'col'=4,'batch'=2] {'seq','col'}, use_global_device_ids=true, to_apply=%region_7.8 | all-reduce | flops 4096 | bytes 32768 | tf_op jit(solution)/shard_map/psum | solution.py:157
  909.0 9.2 psum.15
  (120 shorter events, 42.3 us)
Async XLA Ops:
  7.2 22.7 %copy-start = (bf16[768,1536]{1,0:T(8,128)(2,1)S(1)}, bf16[768,1536]{1,0:T(8,128)(2,1)}, u32[]{:S(2)}) copy-start(bf16[768,1536]{1,0:T(8,128)(2,1)} %param.17) | copy-start | bytes 7077892
  7.2 96.2 %all-gather.2.cloned.1.call-start = ((), (), s32[]{:S(2)}) async-start(), calls=%async_computation.1 | async-start | bytes 1597440 | tf_op jit(solution)/shard_map/all_gather | solution.py:72
  11.8 4.7 collective-permute-start
  15.2 5.5 collective-permute-start.1
  16.5 4.9 slice-start
  17.3 4.2 slice-start.1
  17.4 4.1 copy-start.11
  21.5 8.4 copy-start.6
  21.5 9.0 copy-start.10
  21.5 81.9 %copy-start.5 = (bf16[1536,64]{0,1:T(8,128)(2,1)S(1)}, bf16[1536,64]{0,1:T(8,128)(2,1)}, u32[]{:S(2)}) copy-start(bf16[1536,64]{0,1:T(8,128)(2,1)} %param.19) | copy-start | bytes 589828
  29.9 75.9 %copy-start.4 = (bf16[1024,128]{1,0:T(8,128)(2,1)S(1)}, bf16[1024,128]{1,0:T(8,128)(2,1)}, u32[]{:S(2)}) copy-start(bf16[1024,128]{1,0:T(8,128)(2,1)} %param.20) | copy-start | bytes 786436
  31.2 304.1 %reduce-scatter.4.cloned.1.call-start = ((), (), s32[]{:S(2)}) async-start(), calls=%async_computation.2 | async-start | bytes 3194880 | tf_op jit(solution)/shard_map/reduce_scatter | solution.py:118
  109.5 11.1 %copy-start.1 = (f32[8,128,32,32]{1,3,2,0:T(8,128)S(1)}, f32[8,128,32,32]{1,3,2,0:T(8,128)}, u32[]{:S(2)}) copy-start(f32[8,128,32,32]{1,3,2,0:T(8,128)} %fusion.101) | copy-start | bytes 12582916 | tf_op jit(solution)/shard_map/while
  129.1 11.1 %copy-start.1 = (f32[8,128,32,32]{1,3,2,0:T(8,128)S(1)}, f32[8,128,32,32]{1,3,2,0:T(8,128)}, u32[]{:S(2)}) copy-start(f32[8,128,32,32]{1,3,2,0:T(8,128)} %fusion.101) | copy-start | bytes 12582916 | tf_op jit(solution)/shard_map/while
  148.7 11.1 %copy-start.1 = (f32[8,128,32,32]{1,3,2,0:T(8,128)S(1)}, f32[8,128,32,32]{1,3,2,0:T(8,128)}, u32[]{:S(2)}) copy-start(f32[8,128,32,32]{1,3,2,0:T(8,128)} %fusion.101) | copy-start | bytes 12582916 | tf_op jit(solution)/shard_map/while
  168.3 11.1 %copy-start.1 = (f32[8,128,32,32]{1,3,2,0:T(8,128)S(1)}, f32[8,128,32,32]{1,3,2,0:T(8,128)}, u32[]{:S(2)}) copy-start(f32[8,128,32,32]{1,3,2,0:T(8,128)} %fusion.101) | copy-start | bytes 12582916 | tf_op jit(solution)/shard_map/while
  342.7 12.6 %copy-start.2 = (bf16[1024,768]{1,0:T(8,128)(2,1)}, bf16[1024,768]{1,0:T(8,128)(2,1)S(1)}, u32[]{:S(2)}) copy-start(bf16[1024,768]{1,0:T(8,128)(2,1)S(1)} %fusion.15) | copy-start | bytes 4718596
  355.3 209.1 %collective-permute-start.2 = (bf16[2,768]{1,0:T(2,128)(2,1)S(1)}, bf16[2,768]{1,0:T(2,128)(2,1)S(1)}, u32[]{:S(2)}, u32[]{:S(2)}) collective-permute-start(bf16[2,768]{1,0:T(2,128)(2,1)S(1)} %get-tuple-element.104), channel_id=1, source_target_pairs={{2,0},{4,2},{6,4},{8,6},{10,8},{12,10},{14,12},{16,14},{18,16},{20... | collective-permute-start | bytes 9224 | tf_op jit(solution)/shard_map/ppermute | solution.py:23
  558.3 9.3 %copy-start.3 = (bf16[1024,768]{1,0:T(8,128)(2,1)S(1)}, bf16[1024,768]{1,0:T(8,128)(2,1)}, u32[]{:S(2)}) copy-start(bf16[1024,768]{1,0:T(8,128)(2,1)} %copy-done.2) | copy-start | bytes 4718596
  558.4 18.6 %collective-permute-start.4 = (f32[64,768]{1,0:T(8,128)S(1)}, f32[64,768]{1,0:T(8,128)S(1)}, u32[]{:S(2)}, u32[]{:S(2)}) collective-permute-start(f32[64,768]{1,0:T(8,128)S(1)} %fusion), channel_id=1, source_target_pairs={{0,2},{2,4},{4,6},{6,8},{8,10},{10,12},{12,14},{14,16},{16,18},{18... | collective-permute-start | bytes 589832
  559.8 17.2 %collective-permute-start.5 = (f32[64,768]{1,0:T(8,128)S(1)}, f32[64,768]{1,0:T(8,128)S(1)}, u32[]{:S(2)}, u32[]{:S(2)}) collective-permute-start(f32[64,768]{1,0:T(8,128)S(1)} %fusion), channel_id=1, source_target_pairs={{0,4},{2,6},{4,8},{6,10},{8,12},{10,14},{12,16},{14,18},{16,20},{1... | collective-permute-start | bytes 589832
  561.1 17.3 %collective-permute-start.6 = (f32[64,768]{1,0:T(8,128)S(1)}, f32[64,768]{1,0:T(8,128)}, u32[]{:S(2)}, u32[]{:S(2)}) collective-permute-start(f32[64,768]{1,0:T(8,128)S(1)} %fusion), channel_id=1, source_target_pairs={{0,6},{2,8},{4,10},{6,12},{8,14},{10,16},{12,18},{14,20},{16,22},{... | collective-permute-start | bytes 589832
  563.1 13.9 %collective-permute-start.7 = (f32[60,768]{1,0:T(8,128)S(1)}, f32[60,768]{1,0:T(8,128)S(1)}, u32[]{:S(2)}, u32[]{:S(2)}) collective-permute-start(f32[60,768]{1,0:T(8,128)S(1)} %slice.78), channel_id=1, source_target_pairs={{0,8},{2,10},{4,12},{6,14},{8,16},{10,18},{12,20},{14,22},{16,24},... | collective-permute-start | bytes 552968
  564.4 3.8 collective-permute-start.3
  (6 other events, 10.3 us)
Sparse Core Ops, SparseCore 0:
  31.3 72.0 all-gather.1
  189.8 145.4 reduce-scatter.3
where the time goes:
time: 927 us; the launch traced here: 926 us
  blocking collectives  535 us (58%)
  waiting for transfers between devices  219 us (24%)
  matrix products  118 us (13%)
  between operations  15.9 us (2%)
  starting transfers between devices  13.6 us (1%)
  other arithmetic  13 us (1%)
  local copies, waits for them, and re-layouts  11.9 us (1%)
    psum x1, blocking collectives, shards(): lax.psum(jnp.dot(member, projected, precision=highest), ('seq', 'col'))  324 us
    unnamed x1, blocking collectives  202 us
    reduce_scatter x1, waiting for transfers between devices, shards(): lax.psum_scatter(placed, ('seq', 'col'), scatter_dimension=0, tiled=True)  144 us
    all_gather x1, waiting for transfers between devices, shards(): every = lax.all_gather(normed, ('seq', 'col'), axis=0, tiled=True)  72 us
    dot_general x4, matrix products, pair_step(): jnp.einsum('ijkl,jl->ik', outer_grad, right_wide, precision=highest)  44.3 us
    dot_general x4, matrix products, pair_step(): jnp.einsum('ijkl,ik->jl', outer_grad, rows_left, precision=highest)  18.7 us
  transfers between devices with their start and end apart: 10, of which 3 were waited for; matrix products, arithmetic and copies ran while one was open for 23% of the time, Pallas kernels for 0%

commit v1 on v0

--- a/solution.py
+++ b/solution.py
@@ -154,7 +154,7 @@
     )
     projected = jnp.dot(share, projection, precision=highest)
     member = (labels[None, :] == jnp.arange(BUCKETS, dtype=jnp.int32)[:, None]).astype(jnp.float32)
-    sketch = lax.psum(jnp.dot(member, projected, precision=highest), ("seq", "col"))
+    sketch = lax.psum(lax.psum(jnp.dot(member, projected, precision=highest), "seq"), "col")
     unit = sketch * lax.rsqrt(jnp.mean(sketch * sketch) + 1e-06)
     center = lax.psum(unit, "batch") / lax.axis_size("batch")
     return (input_grad[None], (unit - center)[None])

time: 927 us -> 687 us (0.74)
  blocking collectives: 535 us -> 294 us
    psum x1 -> x2, blocking collectives: 324 us -> 82 us  [the longest x1 67.7 us: shards(): lax.psum(jnp.dot(member, projected, precision=highest), 'seq')]
  transfers between devices with their start and end apart: 10 -> 10, of which waited for: 3 -> 3; matrix products, arithmetic and copies ran while one was open for 23% -> 31% of each run, Pallas kernels for 0% -> 0%
where the time goes in v1:
time: 687 us; the launch traced here: 686 us
  blocking collectives  294 us (43%)
  waiting for transfers between devices  219 us (32%)
  matrix products  118 us (17%)
  between operations  15.9 us (2%)
  starting transfers between devices  14.4 us (2%)
  other arithmetic  13 us (2%)
  local copies, waits for them, and re-layouts  11.9 us (2%)
    unnamed x1, blocking collectives  202 us
    reduce_scatter x1, waiting for transfers between devices, shards(): lax.psum_scatter(placed, ('seq', 'col'), scatter_dimension=0, tiled=True)  144 us
    all_gather x1, waiting for transfers between devices, shards(): every = lax.all_gather(normed, ('seq', 'col'), axis=0, tiled=True)  72 us
    psum x1, blocking collectives, shards(): lax.psum(jnp.dot(member, projected, precision=highest), 'seq')  67.7 us
    dot_general x4, matrix products, pair_step(): jnp.einsum('ijkl,jl->ik', outer_grad, right_wide, precision=highest)  44.3 us
    dot_general x4, matrix products, pair_step(): jnp.einsum('ijkl,ik->jl', outer_grad, rows_left, precision=highest)  18.7 us
    dot_general x4, matrix products, pair_step(): lax.dot_general(block.reshape(bins_dev * col_len, pair_channels), out_wei...  14.5 us
    psum x1, blocking collectives, shards(): lax.psum(lax.psum(jnp.dot(member, projected, precision=highest), 'seq'),...  14.3 us
  transfers between devices with their start and end apart: 10, of which 3 were waited for; matrix products, arithmetic and copies ran while one was open for 31% of the time, Pallas kernels for 0%

profile of v1, /device:TPU:8, one launch (start us, length us, event | category | flops | bytes accessed | tf_op | source)
XLA Modules:
  0.0 685.5 jit_solution(17896756551876458649)
XLA Ops:
  21.5 8.4 %bitcast_reduce_fusion = (f32[8,768]{1,0:T(8,128)S(1)}, f32[1024,768]{1,0:T(8,128)}) fusion(f32[768]{0:T(1024)S(1)} %copy-done.11, bf16[1024,3840]{1,0:T(8,128)(2,1)S(1)} %fusion.34, bf16[3840,768]{1,0:T(8,128)(2,1)S(1)} %bitcast.117), kind=kOutput, calls=%fused_computation.26 | convolution fusion | flops 6047655936 | bytes 16935936 | tf_op jit(solution)/shard_map/dot_general | solution.py:59
  31.4 72.0 %all-gather.2.cloned.1.call-done = bf16[512,1536]{1,0:T(8,128)(2,1)} async-done(((bf16[8,1536]{1,0:T(8,128)(2,1)}), bf16[512,1536]{1,0:T(8,128)(2,1)}) %all-gather.2.cloned.1.call-update) | async-done | bytes 1572880 | tf_op jit(solution)/shard_map/all_gather | solution.py:72
  105.8 78.4 %while.13 = (s32[]{:T(128)}, f32[128,32]{1,0:T(8,128)S(1)}, f32[4,8,32]{2,1,0:T(8,128)S(1)}, bf16[4,8,128,128]{3,2,1,0:T(8,128)(2,1)}, bf16[1024,128]{1,0:T(8,12...) while((s32[]{:T(128)}, f32[128,32]{1,0:T(8,128)S(1)}, ...), condition=%wide.region_3.4_spmd.clone, body=%wide.region_2.3_spmd.clone.sunk | while | flops 293609472 | bytes 30050948 | solution.py:98
  105.8 3.6 fusion.101
  109.5 11.1 %fusion.102 = f32[1,8,32,1]{2,0,3,1:T(1,128)S(1)} fusion(f32[128,32,1,1]{0,2,1,3:T(1,128)S(1)} %copy.35, f32[8,128,32,32]{1,3,2,0:T(8,128)} %fusion.101), kind=kOutput, calls=%fused_computation.clone.1 | convolution fusion | flops 12582912 | bytes 4211712 | tf_op jit(solution)/shard_map/while/body/eval_jaxpr/ijkl,jl->ik/dot_general | solution.py:94
  120.6 4.7 fusion.103
  125.4 3.6 fusion.101
  129.1 11.1 %fusion.102 = f32[1,8,32,1]{2,0,3,1:T(1,128)S(1)} fusion(f32[128,32,1,1]{0,2,1,3:T(1,128)S(1)} %copy.35, f32[8,128,32,32]{1,3,2,0:T(8,128)} %fusion.101), kind=kOutput, calls=%fused_computation.clone.1 | convolution fusion | flops 12582912 | bytes 4211712 | tf_op jit(solution)/shard_map/while/body/eval_jaxpr/ijkl,jl->ik/dot_general | solution.py:94
  140.2 4.7 fusion.103
  145.0 3.6 fusion.101
  148.7 11.1 %fusion.102 = f32[1,8,32,1]{2,0,3,1:T(1,128)S(1)} fusion(f32[128,32,1,1]{0,2,1,3:T(1,128)S(1)} %copy.35, f32[8,128,32,32]{1,3,2,0:T(8,128)} %fusion.101), kind=kOutput, calls=%fused_computation.clone.1 | convolution fusion | flops 12582912 | bytes 4211712 | tf_op jit(solution)/shard_map/while/body/eval_jaxpr/ijkl,jl->ik/dot_general | solution.py:94
  159.8 4.7 fusion.103
  164.6 3.6 fusion.101
  168.3 11.1 %fusion.102 = f32[1,8,32,1]{2,0,3,1:T(1,128)S(1)} fusion(f32[128,32,1,1]{0,2,1,3:T(1,128)S(1)} %copy.35, f32[8,128,32,32]{1,3,2,0:T(8,128)} %fusion.101), kind=kOutput, calls=%fused_computation.clone.1 | convolution fusion | flops 12582912 | bytes 4211712 | tf_op jit(solution)/shard_map/while/body/eval_jaxpr/ijkl,jl->ik/dot_general | solution.py:94
  179.4 4.7 fusion.103
  191.6 143.6 %reduce-scatter.4.cloned.1.call-done = f32[8,1536]{1,0:T(8,128)} async-done(((f32[512,1536]{1,0:T(8,128)}), f32[8,1536]{1,0:T(8,128)}) %reduce-scatter.4.cloned.1.call-update) | async-done | bytes 49168 | tf_op jit(solution)/shard_map/reduce_scatter | solution.py:118
  338.9 3.7 fusion.15
  342.6 12.6 %fusion.70 = f32[3840,768]{1,0:T(8,128)} fusion(bf16[1024,3840]{1,0:T(8,128)(2,1)} %copy-done.6, bf16[1024,768]{1,0:T(8,128)(2,1)S(1)} %fusion.15), kind=kOutput, calls=%fused_computation.110 | convolution fusion | flops 6039797760 | bytes 21233664 | tf_op jit(solution)/shard_map/dot_general | solution.py:145
  356.6 201.8 %fusion = f32[64,768]{1,0:T(8,128)S(1)} fusion(f32[3840,768]{1,0:T(8,128)} %fusion.70), kind=kCustom, calls=%all-reduce-scatter | all-reduce-scatter fusion | flops 3145729 | bytes 11993600
  570.4 7.4 %fusion.36 = bf16[1,1024,768]{2,1,0:T(8,128)(2,1)} fusion(bf16[1024,5,768]{2,0,1:T(8,128)(2,1)S(1)} %fusion.31, bf16[5,768,768]{2,1,0:T(8,128)(2,1)S(1)} %bitcast.120), kind=kOutput, calls=%fused_computation.61 | convolution fusion | flops 6040584192 | bytes 15335424 | tf_op jit(solution)/shard_map/tko,kio->ti/dot_general | solution.py:137
  579.2 4.3 concatenate.26
  585.0 67.7 %psum.21 = f32[32,128]{1,0:T(8,128)S(1)} all-reduce(f32[32,128]{1,0:T(8,128)S(1)} %fusion.60), channel_id=1, replica_groups=mesh['seq'=16,'col'=4,'batch'=2] {'seq'}, use_global_device_ids=true, to_apply=%region_7.8 | all-reduce | flops 4096 | bytes 32768 | tf_op jit(solution)/shard_map/psum | solution.py:157
  652.7 14.3 %psum.22 = f32[32,128]{1,0:T(8,128)S(1)} all-reduce(f32[32,128]{1,0:T(8,128)S(1)} %psum.21), channel_id=1, replica_groups=mesh['seq'=16,'col'=4,'batch'=2] {'col'}, use_global_device_ids=true, to_apply=%region_8.9 | all-reduce | flops 4096 | bytes 32768 | tf_op jit(solution)/shard_map/psum | solution.py:157
  668.3 9.7 %psum.23 = f32[32,128]{1,0:T(8,128)S(1)} all-reduce(f32[32,128]{1,0:T(8,128)S(1)} %broadcast_multiply_fusion), channel_id=1, replica_groups=mesh['seq'=16,'col'=4,'batch'=2] {'batch'}, use_global_device_ids=true, to_apply=%region_10.11 | all-reduce | flops 4096 | bytes 32768 | tf_op jit(solution)/shard_map/psum | solution.py:159
  (121 shorter events, 46.5 us)
Async XLA Ops:
  7.2 22.7 %copy-start = (bf16[768,1536]{1,0:T(8,128)(2,1)S(1)}, bf16[768,1536]{1,0:T(8,128)(2,1)}, u32[]{:S(2)}) copy-start(bf16[768,1536]{1,0:T(8,128)(2,1)} %param.17) | copy-start | bytes 7077892
  7.2 96.2 %all-gather.2.cloned.1.call-start = ((), (), s32[]{:S(2)}) async-start(), calls=%async_computation.1 | async-start | bytes 1597440 | tf_op jit(solution)/shard_map/all_gather | solution.py:72
  11.8 4.7 collective-permute-start
  15.2 5.5 collective-permute-start.1
  16.5 4.9 slice-start
  17.3 4.2 slice-start.1
  17.4 4.1 copy-start.11
  21.5 8.4 %copy-start.6 = (bf16[1024,3840]{1,0:T(8,128)(2,1)}, bf16[1024,3840]{1,0:T(8,128)(2,1)S(1)}, u32[]{:S(2)}) copy-start(bf16[1024,3840]{1,0:T(8,128)(2,1)S(1)} %fusion.34) | copy-start | bytes 23592964
  21.5 9.0 %copy-start.10 = (f32[1536]{0:T(1024)S(1)}, f32[1536]{0:T(1024)}, u32[]{:S(2)}) copy-start(f32[1536]{0:T(1024)} %param.18) | copy-start | bytes 18436
  21.5 81.9 %copy-start.5 = (bf16[1536,64]{0,1:T(8,128)(2,1)S(1)}, bf16[1536,64]{0,1:T(8,128)(2,1)}, u32[]{:S(2)}) copy-start(bf16[1536,64]{0,1:T(8,128)(2,1)} %param.19) | copy-start | bytes 589828
  29.9 75.9 %copy-start.4 = (bf16[1024,128]{1,0:T(8,128)(2,1)S(1)}, bf16[1024,128]{1,0:T(8,128)(2,1)}, u32[]{:S(2)}) copy-start(bf16[1024,128]{1,0:T(8,128)(2,1)} %param.20) | copy-start | bytes 786436
  31.2 304.1 %reduce-scatter.4.cloned.1.call-start = ((), (), s32[]{:S(2)}) async-start(), calls=%async_computation.2 | async-start | bytes 3194880 | tf_op jit(solution)/shard_map/reduce_scatter | solution.py:118
  109.5 11.1 %copy-start.1 = (f32[8,128,32,32]{1,3,2,0:T(8,128)S(1)}, f32[8,128,32,32]{1,3,2,0:T(8,128)}, u32[]{:S(2)}) copy-start(f32[8,128,32,32]{1,3,2,0:T(8,128)} %fusion.101) | copy-start | bytes 12582916 | tf_op jit(solution)/shard_map/while
  129.1 11.1 %copy-start.1 = (f32[8,128,32,32]{1,3,2,0:T(8,128)S(1)}, f32[8,128,32,32]{1,3,2,0:T(8,128)}, u32[]{:S(2)}) copy-start(f32[8,128,32,32]{1,3,2,0:T(8,128)} %fusion.101) | copy-start | bytes 12582916 | tf_op jit(solution)/shard_map/while
  148.7 11.1 %copy-start.1 = (f32[8,128,32,32]{1,3,2,0:T(8,128)S(1)}, f32[8,128,32,32]{1,3,2,0:T(8,128)}, u32[]{:S(2)}) copy-start(f32[8,128,32,32]{1,3,2,0:T(8,128)} %fusion.101) | copy-start | bytes 12582916 | tf_op jit(solution)/shard_map/while
  168.3 11.1 %copy-start.1 = (f32[8,128,32,32]{1,3,2,0:T(8,128)S(1)}, f32[8,128,32,32]{1,3,2,0:T(8,128)}, u32[]{:S(2)}) copy-start(f32[8,128,32,32]{1,3,2,0:T(8,128)} %fusion.101) | copy-start | bytes 12582916 | tf_op jit(solution)/shard_map/while
  342.6 12.6 %copy-start.2 = (bf16[1024,768]{1,0:T(8,128)(2,1)}, bf16[1024,768]{1,0:T(8,128)(2,1)S(1)}, u32[]{:S(2)}) copy-start(bf16[1024,768]{1,0:T(8,128)(2,1)S(1)} %fusion.15) | copy-start | bytes 4718596
  355.3 209.4 %collective-permute-start.2 = (bf16[2,768]{1,0:T(2,128)(2,1)S(1)}, bf16[2,768]{1,0:T(2,128)(2,1)S(1)}, u32[]{:S(2)}, u32[]{:S(2)}) collective-permute-start(bf16[2,768]{1,0:T(2,128)(2,1)S(1)} %get-tuple-element.104), channel_id=1, source_target_pairs={{2,0},{4,2},{6,4},{8,6},{10,8},{12,10},{14,12},{16,14},{18,16},{20... | collective-permute-start | bytes 9224 | tf_op jit(solution)/shard_map/ppermute | solution.py:23
  558.3 10.2 %copy-start.3 = (bf16[1024,768]{1,0:T(8,128)(2,1)S(1)}, bf16[1024,768]{1,0:T(8,128)(2,1)}, u32[]{:S(2)}) copy-start(bf16[1024,768]{1,0:T(8,128)(2,1)} %copy-done.2) | copy-start | bytes 4718596
  558.4 19.4 %collective-permute-start.4 = (f32[64,768]{1,0:T(8,128)S(1)}, f32[64,768]{1,0:T(8,128)S(1)}, u32[]{:S(2)}, u32[]{:S(2)}) collective-permute-start(f32[64,768]{1,0:T(8,128)S(1)} %fusion), channel_id=1, source_target_pairs={{0,2},{2,4},{4,6},{6,8},{8,10},{10,12},{12,14},{14,16},{16,18},{18... | collective-permute-start | bytes 589832
  560.0 17.8 %collective-permute-start.5 = (f32[64,768]{1,0:T(8,128)S(1)}, f32[64,768]{1,0:T(8,128)S(1)}, u32[]{:S(2)}, u32[]{:S(2)}) collective-permute-start(f32[64,768]{1,0:T(8,128)S(1)} %fusion), channel_id=1, source_target_pairs={{0,4},{2,6},{4,8},{6,10},{8,12},{10,14},{12,16},{14,18},{16,20},{1... | collective-permute-start | bytes 589832
  561.3 17.9 %collective-permute-start.6 = (f32[64,768]{1,0:T(8,128)S(1)}, f32[64,768]{1,0:T(8,128)}, u32[]{:S(2)}, u32[]{:S(2)}) collective-permute-start(f32[64,768]{1,0:T(8,128)S(1)} %fusion), channel_id=1, source_target_pairs={{0,6},{2,8},{4,10},{6,12},{8,14},{10,16},{12,18},{14,20},{16,22},{... | collective-permute-start | bytes 589832
  563.3 14.5 %collective-permute-start.7 = (f32[60,768]{1,0:T(8,128)S(1)}, f32[60,768]{1,0:T(8,128)S(1)}, u32[]{:S(2)}, u32[]{:S(2)}) collective-permute-start(f32[60,768]{1,0:T(8,128)S(1)} %slice.78), channel_id=1, source_target_pairs={{0,8},{2,10},{4,12},{6,14},{8,16},{10,18},{12,20},{14,22},{16,24},... | collective-permute-start | bytes 552968
  564.6 4.4 collective-permute-start.3
  (6 other events, 10.3 us)
Sparse Core Ops, SparseCore 0:
  31.3 72.0 all-gather.1
  189.7 145.5 reduce-scatter.3
